TPU v7x, 128 devices: a whole 4x4x4 slice. The times are simulated.
128 devices in a mesh: row: 8 (over z, core), col: 16 (over x, y).
Axes of the slice: x: 4, y: 4, z: 4, core: 2. Of those that a mesh axis runs over, the one named last changes fastest.
Arguments:
- hessian_inverse: float32 [12288, 12288], P('row', 'col'), as said below
- weight: bfloat16 [12288, 4096], P('row', 'col'), may hold values from -6 to 6
- pruned: int32 [2, 512], replicated, may hold values from 0 to 12287, as said below
Outputs:
- hessian_after: float32 [12288, 12288], P('row', 'col')
- weight_after: bfloat16 [12288, 4096], P('row', 'col')
Inputs may be any that keep to these rules, and one draw needn't show every extreme that they name: `hessian_inverse`: symmetric and positive definite. `pruned`: all 1024 channel numbers are distinct.
All inputs are finite; a program needn't handle non-finite values.
Results may differ from a plain program's by a relative error of at most 0.001.
Values sent between devices are 32-bit elements; how exact they have to be, the bound alone decides.
No kernel may reach another device: no remote copies, remote signals or barrier semaphores. Data moves between devices by JAX's collectives and lax.ppermute only.
A program may use at most 128 MiB of HBM per device.

v0:
```python
import jax
import jax.numpy as jnp
from jax import lax
from jax.sharding import PartitionSpec as P

PANELS = 2


def contract_rows(gains, rows):
    return lax.dot_general(
        gains,
        rows,
        (((0,), (0,)), ((), ())),
        precision=lax.Precision.HIGHEST,
        preferred_element_type=jnp.float32,
    )


def solve_pivot(factor, rhs):
    half = lax.linalg.triangular_solve(factor, rhs, left_side=True, lower=True)
    return lax.linalg.triangular_solve(factor, half, left_side=True, lower=True, transpose_a=True)


def locate(listed, start, count):
    local_ids = listed - start
    valid = (local_ids >= 0) & (local_ids < count)
    clipped = jnp.clip(local_ids, 0, count - 1)
    marked = jnp.zeros((count,), jnp.float32).at[clipped].max(valid.astype(jnp.float32)) > 0.5
    return (clipped, valid, marked)


def per_device(hessian_inverse, weight, pruned):
    row_count = hessian_inverse.shape[0]
    col_count = hessian_inverse.shape[1]
    row_start = lax.axis_index("row") * row_count
    col_start = lax.axis_index("col") * col_count
    inverse = hessian_inverse
    slab = weight.astype(jnp.float32)
    for panel in range(PANELS):
        listed = pruned[panel]
        row_pick, row_valid, row_marked = locate(listed, row_start, row_count)
        col_pick, col_valid, col_marked = locate(listed, col_start, col_count)
        mine_rows = jnp.where(row_valid[:, None], jnp.take(inverse, row_pick, axis=0), 0.0)
        mine_slab = jnp.where(row_valid[:, None], jnp.take(slab, row_pick, axis=0), 0.0)
        panel_rows, slab_rows = lax.psum((mine_rows, mine_slab), "row")
        panel_pivot = jnp.where(col_valid[None, :], jnp.take(panel_rows, col_pick, axis=1), 0.0)
        pivot = lax.psum(panel_pivot, "col")
        factor = jnp.linalg.cholesky(pivot)
        mine_cols = jnp.where(col_valid[None, :], jnp.take(inverse, col_pick, axis=1), 0.0)
        columns = lax.psum(mine_cols, "col")
        gains = solve_pivot(factor, columns.T)
        slab = slab - contract_rows(gains, slab_rows)
        slab = jnp.where(row_marked[:, None], 0.0, slab)
        inverse = inverse - contract_rows(gains, panel_rows)
        inverse = jnp.where(row_marked[:, None] | col_marked[None, :], 0.0, inverse)
    return (inverse, slab.astype(jnp.bfloat16))


def solution(mesh):
    in_specs = (P("row", "col"), P("row", "col"), P())
    out_specs = (P("row", "col"), P("row", "col"))
    return jax.shard_map(
        per_device, mesh=mesh, in_specs=in_specs, out_specs=out_specs, check_vma=False
    )
```

profile of v0, /device:TPU:1, one launch (start us, length us, event | category | flops | bytes accessed | tf_op | source)
XLA Modules:
  0.0 719.2 jit_solution(886581179572580454)
XLA Ops:
  33.8 53.3 %all-reduce.16.cloned.1.call-done = (f32[512,768]{1,0:T(8,128)}, f32[512,256]{1,0:T(8,128)}) async-done(((f32[512,768]{1,0:T(8,128)}, f32[512,256]{1,0:T(8,128)}), (f32[512,768]{1,0:T(8,128)}, f32[512,256]{1,0:T(8,128)})) %all-reduce.16.cloned.1.call-update) | async-done | bytes 2097168 | tf_op jit(solution)/shard_map/psum | solution.py:45
  99.8 96.6 %all-reduce.12.cloned.1.call-done = (f32[512,1536]{1,0:T(8,128)}, f32[512,512]{0,1:T(8,128)}) async-done(((f32[512,1536]{1,0:T(8,128)}, f32[512,512]{0,1:T(8,128)}), (f32[512,1536]{1,0:T(8,128)}, f32[512,512]{0,1:T(8,128)})) %all-reduce.12.cloned.1.call-update) | async-done | bytes 4194320 | tf_op jit(solution)/shard_map/psum | solution.py:50
  198.3 11.7 %cholesky.286 = f32[128,128]{1,0:T(8,128)S(1)} custom-call(f32[128,128]{1,0:T(8,128)S(1)} %cholesky.426), custom_call_target="Cholesky" | custom-call | tf_op jit(solution)/shard_map/jit(cholesky)/cholesky | solution.py:48
  210.2 9.8 %custom-call.31 = f32[1,128,128]{1,2,0:T(8,128)S(1)} custom-call(f32[1,128,128]{2,1,0:T(8,128)S(1)} %get-tuple-element.100), custom_call_target="InvertDiagBlocksLowerTriangular" | custom-call | tf_op jit(solution)/shard_map/jit(cholesky)/cholesky | solution.py:48
  220.6 11.7 %cholesky.305 = f32[128,128]{1,0:T(8,128)S(1)} custom-call(f32[128,128]{1,0:T(8,128)S(1)} %cholesky.430), custom_call_target="Cholesky" | custom-call | tf_op jit(solution)/shard_map/jit(cholesky)/cholesky | solution.py:48
  232.4 10.2 %custom-call.32 = f32[1,128,128]{1,2,0:T(8,128)S(1)} custom-call(f32[1,128,128]{2,1,0:T(8,128)S(1)} %get-tuple-element.97), custom_call_target="InvertDiagBlocksLowerTriangular" | custom-call | tf_op jit(solution)/shard_map/jit(cholesky)/cholesky | solution.py:48
  243.2 11.7 %cholesky.326 = f32[128,128]{1,0:T(8,128)S(1)} custom-call(f32[128,128]{1,0:T(8,128)S(1)} %cholesky.435), custom_call_target="Cholesky" | custom-call | tf_op jit(solution)/shard_map/jit(cholesky)/cholesky | solution.py:48
  255.0 9.8 %custom-call.33 = f32[1,128,128]{1,2,0:T(8,128)S(1)} custom-call(f32[1,128,128]{2,1,0:T(8,128)S(1)} %get-tuple-element.94), custom_call_target="InvertDiagBlocksLowerTriangular" | custom-call | tf_op jit(solution)/shard_map/jit(cholesky)/cholesky | solution.py:48
  265.4 11.7 %cholesky.343 = f32[128,128]{1,0:T(8,128)S(1)} custom-call(f32[128,128]{1,0:T(8,128)S(1)} %convolution_subtract_fusion.19), custom_call_target="Cholesky" | custom-call | tf_op jit(solution)/shard_map/jit(cholesky)/cholesky | solution.py:48
  282.0 7.6 %while.8 = (s32[]{:T(128)}, f32[512,512]{1,0:T(8,128)S(1)}, s32[4,2]{0,1:T(2,128)S(1)}, f32[4,128,128]{2,1,0:T(8,128)S(1)}, s32[]{:T(128)}) while((s32[]{:T(128)}, f32[512,512]{1,0:T(8,128)S(1)}, s32[4,2]{0,1:T(2,128)S(1)}, f32[4,128,128]{2,1,0:T(8,128)S(1)}, s32[]{:T(128)}) %tuple.80), condition=%wide.while_cond.1, body=%wide.while_body.1.sunk | while | flops 2 | bytes 131189 | solution.py:21
  289.6 39.3 %custom-call.35 = f32[4,128,128]{1,2,0:T(8,128)S(1)} custom-call(f32[4,128,128]{2,1,0:T(8,128)S(1)} %get-tuple-element.38), custom_call_target="InvertDiagBlocksLowerTriangular" | custom-call | tf_op jit(solution)/shard_map/triangular_solve/custom-call.8 | solution.py:21
  345.3 10.7 %subtract_select_fusion.1 = f32[1536,768]{1,0:T(8,128)} fusion(f32[1536,768]{1,0:T(8,128)S(1)} %bitcast.167, f32[512,768]{1,0:T(8,128)S(1)} %copy-done.2, pred[768]{0:T(1024)(128)(4,1)S(1)} %broadcast_compare_fusion.2, pred[1536]{0:T(1024)(128)(4,1)S(1)} %broadcast_compare_fusion, f32[128,1536]{1,0:T(8,128)S(1)} %fusion.83, f32[128,1536]{1,0:T(8,128)S(1)} %fusion.81, ...), kind=kOutput, calls=%fused_computation.17 | convolution fusion | flops 7253655552 | bytes 14158080 | tf_op jit(solution)/shard_map/dot_general | solution.py:10
  385.8 50.2 %all-reduce.14.cloned.1.call-done = (f32[512,768]{1,0:T(8,128)}, f32[512,256]{1,0:T(8,128)}) async-done(((f32[512,768]{1,0:T(8,128)}, f32[512,256]{1,0:T(8,128)}), (f32[512,768]{1,0:T(8,128)}, f32[512,256]{1,0:T(8,128)})) %all-reduce.14.cloned.1.call-update) | async-done | bytes 2097168 | tf_op jit(solution)/shard_map/psum | solution.py:45
  448.5 96.7 %all-reduce.10.cloned.1.call-done = (f32[512,1536]{1,0:T(8,128)}, f32[512,512]{0,1:T(8,128)}) async-done(((f32[512,1536]{1,0:T(8,128)}, f32[512,512]{0,1:T(8,128)}), (f32[512,1536]{1,0:T(8,128)}, f32[512,512]{0,1:T(8,128)})) %all-reduce.10.cloned.1.call-update) | async-done | bytes 4194320 | tf_op jit(solution)/shard_map/psum | solution.py:50
  547.2 11.7 %cholesky.358 = f32[128,128]{1,0:T(8,128)S(1)} custom-call(f32[128,128]{1,0:T(8,128)S(1)} %cholesky.439), custom_call_target="Cholesky" | custom-call | tf_op jit(solution)/shard_map/jit(cholesky)/cholesky | solution.py:48
  559.0 9.8 %custom-call.36 = f32[1,128,128]{1,2,0:T(8,128)S(1)} custom-call(f32[1,128,128]{2,1,0:T(8,128)S(1)} %get-tuple-element.90), custom_call_target="InvertDiagBlocksLowerTriangular" | custom-call | tf_op jit(solution)/shard_map/jit(cholesky)/cholesky | solution.py:48
  569.5 11.7 %cholesky.377 = f32[128,128]{1,0:T(8,128)S(1)} custom-call(f32[128,128]{1,0:T(8,128)S(1)} %cholesky.443), custom_call_target="Cholesky" | custom-call | tf_op jit(solution)/shard_map/jit(cholesky)/cholesky | solution.py:48
  581.3 10.2 %custom-call.37 = f32[1,128,128]{1,2,0:T(8,128)S(1)} custom-call(f32[1,128,128]{2,1,0:T(8,128)S(1)} %get-tuple-element.87), custom_call_target="InvertDiagBlocksLowerTriangular" | custom-call | tf_op jit(solution)/shard_map/jit(cholesky)/cholesky | solution.py:48
  592.1 11.7 %cholesky.398 = f32[128,128]{1,0:T(8,128)S(1)} custom-call(f32[128,128]{1,0:T(8,128)S(1)} %cholesky.448), custom_call_target="Cholesky" | custom-call | tf_op jit(solution)/shard_map/jit(cholesky)/cholesky | solution.py:48
  603.9 9.8 %custom-call.38 = f32[1,128,128]{1,2,0:T(8,128)S(1)} custom-call(f32[1,128,128]{2,1,0:T(8,128)S(1)} %get-tuple-element.84), custom_call_target="InvertDiagBlocksLowerTriangular" | custom-call | tf_op jit(solution)/shard_map/jit(cholesky)/cholesky | solution.py:48
  614.3 11.7 %cholesky.415 = f32[128,128]{1,0:T(8,128)S(1)} custom-call(f32[128,128]{1,0:T(8,128)S(1)} %convolution_subtract_fusion.18), custom_call_target="Cholesky" | custom-call | tf_op jit(solution)/shard_map/jit(cholesky)/cholesky | solution.py:48
  631.7 8.1 %while.9 = (s32[]{:T(128)}, f32[512,512]{1,0:T(8,128)S(1)}, s32[4,2]{0,1:T(2,128)S(1)}, f32[4,128,128]{2,1,0:T(8,128)S(1)}, s32[]{:T(128)}) while((s32[]{:T(128)}, f32[512,512]{1,0:T(8,128)S(1)}, s32[4,2]{0,1:T(2,128)S(1)}, f32[4,128,128]{2,1,0:T(8,128)S(1)}, s32[]{:T(128)}) %tuple.98), condition=%wide.while_cond.1.clone, body=%wide.while_body.1.clone.sunk | while | flops 2 | bytes 131189 | solution.py:21
  639.8 39.3 %custom-call.40 = f32[4,128,128]{1,2,0:T(8,128)S(1)} custom-call(f32[4,128,128]{2,1,0:T(8,128)S(1)} %get-tuple-element.40), custom_call_target="InvertDiagBlocksLowerTriangular" | custom-call | tf_op jit(solution)/shard_map/triangular_solve/custom-call.8 | solution.py:21
  695.3 10.7 %subtract_select_fusion = f32[1536,768]{1,0:T(8,128)} fusion(f32[1536,768]{1,0:T(8,128)S(1)} %bitcast.165, f32[512,768]{1,0:T(8,128)S(1)} %copy-done.3, pred[768]{0:T(1024)(128)(4,1)S(1)} %broadcast_compare_fusion.3, pred[1536]{0:T(1024)(128)(4,1)S(1)} %broadcast_compare_fusion.1, f32[128,1536]{1,0:T(8,128)S(1)} %fusion.90, f32[128,1536]{1,0:T(8,128)S(1)} %fusion.88, ...), kind=kOutput, calls=%fused_computation.16 | convolution fusion | flops 7253655552 | bytes 14158080 | tf_op jit(solution)/shard_map/dot_general | solution.py:10
  (190 shorter events, 148.9 us)
Async XLA Ops:
  7.2 79.9 %all-reduce.16.cloned.1.call-start = ((), (), s32[]{:S(2)}) async-start(), calls=%async_computation.3 | async-start | bytes 4194304 | tf_op jit(solution)/shard_map/psum | solution.py:45
  17.2 1.4 copy-start.8
  19.6 176.8 %all-reduce.12.cloned.1.call-start = ((), (), s32[]{:S(2)}) async-start(), calls=%async_computation.1 | async-start | bytes 8388608 | tf_op jit(solution)/shard_map/psum | solution.py:50
  91.8 344.2 %all-reduce.14.cloned.1.call-start = ((), (), s32[]{:S(2)}) async-start(), calls=%async_computation.2 | async-start | bytes 4194304 | tf_op jit(solution)/shard_map/psum | solution.py:45
  196.4 1.7 copy-start.4
  330.9 2.9 copy-start.6
  338.2 7.0 slice-start.2
  340.6 4.6 slice-start.3
  342.4 2.8 copy-start.2
  345.2 10.7 %copy-start.10 = (bf16[1536,256]{1,0:T(8,128)(2,1)S(1)}, bf16[1536,256]{1,0:T(8,128)(2,1)}, u32[]{:S(2)}) copy-start(bf16[1536,256]{1,0:T(8,128)(2,1)} %param.17) | copy-start | bytes 2359300
  345.3 10.7 %copy-start.11 = (f32[512,256]{1,0:T(8,128)S(1)}, f32[512,256]{1,0:T(8,128)}, u32[]{:S(2)}) copy-start(f32[512,256]{1,0:T(8,128)} %get-tuple-element.68) | copy-start | bytes 1572868
  361.5 5.4 copy-start
  369.1 1.4 copy-start.9
  371.5 173.7 %all-reduce.10.cloned.1.call-start = ((), (), s32[]{:S(2)}) async-start(), calls=%async_computation | async-start | bytes 8388608 | tf_op jit(solution)/shard_map/psum | solution.py:50
  545.2 1.7 copy-start.5
  681.1 2.9 copy-start.7
  688.3 6.9 slice-start
  690.8 4.4 slice-start.1
  692.6 2.6 copy-start.3
  695.2 10.7 %copy-start.1 = (f32[1536,256]{1,0:T(8,128)S(1)}, f32[1536,256]{1,0:T(8,128)}, u32[]{:S(2)}) copy-start(f32[1536,256]{1,0:T(8,128)} %copy-done) | copy-start | bytes 4718596
  695.3 10.7 %copy-start.12 = (f32[512,256]{1,0:T(8,128)S(1)}, f32[512,256]{1,0:T(8,128)}, u32[]{:S(2)}) copy-start(f32[512,256]{1,0:T(8,128)} %get-tuple-element.66) | copy-start | bytes 1572868
Sparse Core Ops, SparseCore 0:
  19.7 67.3 all-reduce.15
  92.0 104.3 all-reduce.11
  371.7 64.2 all-reduce.13
  440.8 104.3 all-reduce.9
where the time goes:
time: 726 us; the launch traced here: 719 us
  waiting for transfers between devices  297 us (41%)
  other arithmetic  268 us (37%)
  matrix products  69.1 us (10%)
  local copies, waits for them, and re-layouts  65 us (9%)
  between operations  20.1 us (3%)
    psum x2, waiting for transfers between devices, per_device(): columns = lax.psum(mine_cols, 'col')  193 us
    another operation x29, other arithmetic, per_device(): factor = jnp.linalg.cholesky(pivot)  158 us
    psum x2, waiting for transfers between devices, per_device(): panel_rows, slab_rows = lax.psum((mine_rows, mine_slab), 'row')  104 us
    another operation x5, other arithmetic, solve_pivot(): lax.linalg.triangular_solve(factor, half, left_side=True, lower=True, tra...  79.2 us
    dot_general x4, matrix products, contract_rows(): lax.dot_general(gains, rows, (((0,), (0,)), ((), ())), precision=lax.Prec...  33.4 us
    another operation x14, matrix products, solve_pivot(): half = lax.linalg.triangular_solve(factor, rhs, left_side=True, lower=True)  18.3 us
    another operation x27, local copies, waits for them, and re-layouts, solve_pivot(): lax.linalg.triangular_solve(factor, half, left_side=True, lower=True, tra...  15.6 us
    another operation x4, other arithmetic, locate(): jnp.zeros((count,), jnp.float32).at[clipped].max(valid.astype(jnp.float32))  15.5 us
  transfers between devices with their start and end apart: 4, of which 4 were waited for; matrix products, arithmetic and copies ran while one was open for 6% of the time, Pallas kernels for 0%

commit v1 on v0

v1 whole, which is shorter than its diff:
```python
import functools

import jax
import jax.numpy as jnp
from jax import lax
from jax.experimental import pallas as pl
from jax.experimental.pallas import tpu as pltpu
from jax.sharding import PartitionSpec as P

NB = 128
f32 = jnp.float32
bf16 = jnp.bfloat16


def split(x):
    high = x.astype(bf16)
    return high, (x - high.astype(f32)).astype(bf16)


def dot3(a, b):
    def one(p, q):
        return lax.dot_general(p, q, (((1,), (0,)), ((), ())), preferred_element_type=f32)

    return one(a[0], b[0]) + (one(a[0], b[1]) + one(a[1], b[0]))


def inverse_of_block(D):
    lane = lax.broadcasted_iota(jnp.int32, (8, 128), 1)
    sub = lax.broadcasted_iota(jnp.int32, (8, 128), 0)
    for s in range(16):
        R = D[s]
        inside = (lane >= 8 * s) & (lane < 8 * s + 8)
        cols = [jnp.broadcast_to(R[:, 8 * s + j : 8 * s + j + 1], (8, 128)) for j in range(8)]
        e = {(i, j): jnp.broadcast_to(cols[j][i : i + 1, :], (8, 128)) for i in range(8) for j in range(i, 8)}
        r = [
            jnp.where(inside, jnp.where(lane == 8 * s + i, 1.0, 0.0), jnp.broadcast_to(R[i : i + 1, :], (8, 128)))
            for i in range(8)
        ]
        for k in range(8):
            inv = 1.0 / e[k, k]
            raw = {j: e[k, j] for j in range(k, 8)}
            r[k] = r[k] * inv
            scaled = {j: e[k, j] * inv for j in range(k + 1, 8)}
            for i in range(8):
                if i == k:
                    continue
                f = e[i, k] if i < k else raw[i]
                r[i] = r[i] - f * r[k]
                for j in range(max(k + 1, i), 8):
                    e[i, j] = e[i, j] - f * scaled[j]
            for j in range(k + 1, 8):
                e[k, j] = scaled[j]
        U = r[7]
        for i in range(7):
            U = jnp.where(sub == i, r[i], U)
        for b in range(16):
            if b == s:
                continue
            C = D[b]
            acc = jnp.where(inside, 0.0, C)
            for j in range(8):
                acc = acc - jnp.broadcast_to(C[:, 8 * s + j : 8 * s + j + 1], (8, 128)) * r[j]
            D[b] = acc
        D[s] = U
    return D


def inverse_kernel(blocks, m_ref, o_ref):
    o_ref[...] = m_ref[...]

    def body(k, _):
        o = pl.multiple_of(k * NB, NB)
        here = pl.ds(o, NB)
        D = inverse_of_block([o_ref[pl.ds(o + 8 * b, 8), here] for b in range(16)])
        D = jnp.concatenate(D, axis=0)
        o_ref[here, here] = jnp.zeros((NB, NB), f32)
        d = split(D)
        U = dot3(d, split(o_ref[here, :]))
        o_ref[here, :] = U
        u = split(U)

        def rows(i, _):
            @pl.when(i != k)
            def _():
                there = pl.ds(pl.multiple_of(i * NB, NB), NB)
                c = split(o_ref[there, here])
                o_ref[there, here] = jnp.zeros((NB, NB), f32)
                o_ref[there, :] = o_ref[there, :] - dot3(c, u)
                o_ref[there, here] = -dot3(c, d)

            return 0

        lax.fori_loop(0, blocks, rows, 0)
        o_ref[here, here] = D
        return 0

    lax.fori_loop(0, blocks, body, 0)


def invert(m):
    n = m.shape[0]
    return pl.pallas_call(
        functools.partial(inverse_kernel, n // NB),
        out_shape=jax.ShapeDtypeStruct((n, n), f32),
        in_specs=[pl.BlockSpec(memory_space=pltpu.VMEM)],
        out_specs=pl.BlockSpec(memory_space=pltpu.VMEM),
        compiler_params=pltpu.CompilerParams(vmem_limit_bytes=32 << 20),
        name="invert",
    )(m)


def dot_high(a, b, contract):
    return lax.dot_general(a, b, (contract, ((), ())), precision=lax.Precision.HIGH, preferred_element_type=f32)


def per_device(hessian_inverse, weight, pruned):
    rows, cols = hessian_inverse.shape
    listed = pruned.reshape(-1)
    row_ids = listed - lax.axis_index("row") * rows
    col_ids = listed - lax.axis_index("col") * cols
    row_ok = (row_ids >= 0) & (row_ids < rows)
    col_ok = (col_ids >= 0) & (col_ids < cols)
    row_marked = jnp.any(row_ids[None, :] == jnp.arange(rows)[:, None], axis=1)
    col_marked = jnp.any(col_ids[None, :] == jnp.arange(cols)[:, None], axis=1)
    row_pick = jnp.clip(row_ids, 0, rows - 1)
    col_pick = jnp.clip(col_ids, 0, cols - 1)
    mine = jnp.where(row_ok[:, None], jnp.take(hessian_inverse, row_pick, axis=0), 0.0)
    slab = jnp.where(row_ok[:, None], jnp.take(weight.astype(f32), row_pick, axis=0), 0.0)
    right = lax.psum(jnp.concatenate([mine, slab], axis=1), "row")
    pivot = lax.psum(jnp.where(col_ok[None, :], jnp.take(right[:, :cols], col_pick, axis=1), 0.0), "col")
    left = lax.psum(jnp.where(col_ok[None, :], jnp.take(hessian_inverse, col_pick, axis=1), 0.0), "col")
    solved = dot_high(invert(pivot), right, ((1,), (0,)))
    update = dot_high(left, solved, ((1,), (0,)))
    inverse = jnp.where(row_marked[:, None] | col_marked[None, :], 0.0, hessian_inverse - update[:, :cols])
    slab = jnp.where(row_marked[:, None], 0.0, weight.astype(f32) - update[:, cols:])
    return inverse, slab.astype(bf16)


def solution(mesh):
    in_specs = (P("row", "col"), P("row", "col"), P())
    out_specs = (P("row", "col"), P("row", "col"))
    return jax.shard_map(per_device, mesh=mesh, in_specs=in_specs, out_specs=out_specs, check_vma=False)
```

time: 726 us -> 375 us (0.52)
  other arithmetic: 268 us -> 22.8 us
  waiting for transfers between devices: 297 us -> 212 us
  Pallas kernels: 0 us -> 62.2 us
  matrix products: 69.1 us -> 17.1 us
  local copies, waits for them, and re-layouts: 65 us -> 46.9 us
    another operation x38 -> x0, other arithmetic: 253 us -> none  [the longest x29 158 us: per_device(): factor = jnp.linalg.cholesky(pivot)]
    psum x4 -> x2, waiting for transfers between devices: 297 us -> 211 us  [the longest x1 159 us: per_device(): lax.psum(jnp.where(col_ok[None, :], jnp.take(hessian_inverse, col_pick, a...]
    pallas_call x0 -> x1, Pallas kernels: none -> 62.2 us  [invert(): pl.pallas_call(functools.partial(inverse_kernel, n // NB), out_shape=jax....]
    another operation x40 -> x0, matrix products: 35.7 us -> none  [the longest x14 18.3 us: solve_pivot(): half = lax.linalg.triangular_solve(factor, rhs, left_side=True, lower=True)]
    dot_general x4 -> x2, matrix products: 33.4 us -> 17.1 us  [dot_high(): lax.dot_general(a, b, (contract, ((), ())), precision=lax.Precision.HIGH,...]
    another operation x35 -> x0, local copies, waits for them, and re-layouts: 15.9 us -> none  [the longest x27 15.6 us: solve_pivot(): lax.linalg.triangular_solve(factor, half, left_side=True, lower=True, tra...]
    select_n x11 -> x7, other arithmetic: 7.97 us -> 15.8 us  [the longest x1 5.35 us: per_device(): jnp.where(col_ok[None, :], jnp.take(hessian_inverse, col_pick, axis=1), 0.0)]
    gather x8 -> x5, local copies, waits for them, and re-layouts: 30 us -> 32.5 us  [the longest x2 10.7 us: per_device(): jnp.take(right[:, :cols], col_pick, axis=1)]
  transfers between devices with their start and end apart: 4 -> 2, of which waited for: 4 -> 2; matrix products, arithmetic and copies ran while one was open for 6% -> 6% of each run, Pallas kernels for 0% -> 0%
where the time goes in v1:
time: 375 us
  waiting for transfers between devices  212 us (57%)
  Pallas kernels  62.2 us (17%)
  local copies, waits for them, and re-layouts  46.9 us (13%)
  other arithmetic  22.8 us (6%)
  matrix products  17.1 us (5%)
  between operations  14.2 us (4%)
    psum x1, waiting for transfers between devices, per_device(): lax.psum(jnp.where(col_ok[None, :], jnp.take(hessian_inverse, col_pick, a...  159 us
    pallas_call x1, Pallas kernels, invert(): pl.pallas_call(functools.partial(inverse_kernel, n // NB), out_shape=jax....  62.2 us
    psum x1, waiting for transfers between devices, per_device(): right = lax.psum(jnp.concatenate([mine, slab], axis=1), 'row')  52.6 us
    dot_general x2, matrix products, dot_high(): lax.dot_general(a, b, (contract, ((), ())), precision=lax.Precision.HIGH,...  17.1 us
    gather x2, local copies, waits for them, and re-layouts, per_device(): jnp.take(right[:, :cols], col_pick, axis=1)  10.7 us
    gather x1, local copies, waits for them, and re-layouts, per_device(): jnp.take(hessian_inverse, col_pick, axis=1)  10.2 us
    unnamed x19, local copies, waits for them, and re-layouts  8.28 us
  transfers between devices with their start and end apart: 2, of which 2 were waited for; matrix products, arithmetic and copies ran while one was open for 6% of the time, Pallas kernels for 0%

profile of v1, /device:TPU:1, one launch (start us, length us, event | category | flops | bytes accessed | tf_op | source)
XLA Modules:
  0.0 374.8 jit_solution(5048881604577638534)
XLA Ops:
  7.2 0.7 subtract_bitcast_fusion.1
  8.0 1.2 convert_element_type.7
  9.2 4.7 %gather_fusion.2 = f32[1024,256]{1,0:T(8,128)} fusion(f32[1536,256]{1,0:T(8,128)S(1)} %convert_element_type.7, s32[1024]{0:T(1024)S(1)} %broadcast_clamp_fusion), kind=kCustom, calls=%fused_computation.2 | custom fusion | bytes 2101248 | tf_op jit(solution)/shard_map/jit(_take)/gather | solution.py:128
  13.9 6.9 %gather_fusion.1 = f32[1024,768]{1,0:T(8,128)S(1)} fusion(f32[1536,768]{1,0:T(8,128)} %param.3, s32[1024]{0:T(1024)S(1)} %broadcast_clamp_fusion), kind=kCustom, calls=%fused_computation.1 | custom fusion | bytes 6295552 | tf_op jit(solution)/shard_map/jit(_take)/gather | solution.py:127
  20.8 1.6 select_select_fusion.1
  22.4 1.0 select_select_fusion
  23.4 2.6 pad_maximum_fusion
  26.0 6.0 %copy.8 = f32[1536,768]{0,1:T(8,128)} copy(f32[1536,768]{1,0:T(8,128)} %param.3) | data formatting | bytes 9437184 | tf_op args[0]
  32.1 10.2 %gather_fusion = f32[1024,1536]{1,0:T(8,128)} fusion(f32[1536,768]{0,1:T(8,128)} %copy.8, s32[1024]{0:T(1024)S(1)} %broadcast_clamp_fusion.1), kind=kCustom, calls=%fused_computation | custom fusion | bytes 12587008 | tf_op jit(solution)/shard_map/jit(_take)/gather | solution.py:131
  42.3 5.3 %select_bitcast_fusion = f32[1536,1024]{0,1:T(8,128)} fusion(f32[1024,1536]{1,0:T(8,128)} %gather_fusion, pred[1024]{0:T(1024)(128)(4,1)S(1)} %get-tuple-element.11, pred[1024]{0:T(1024)(128)(4,1)S(1)} %get-tuple-element.10), kind=kLoop, calls=%fused_computation.4 | loop fusion | flops 3145728 | bytes 12584960 | tf_op jit(solution)/shard_map/jit(_where)/select_n | solution.py:131
  47.7 52.6 %all-reduce.4.cloned.1.call-done = f32[1024,1024]{1,0:T(8,128)} async-done(((f32[1024,1024]{1,0:T(8,128)}), f32[1024,1024]{1,0:T(8,128)}) %all-reduce.4.cloned.1.call-update) | async-done | bytes 4194320 | tf_op jit(solution)/shard_map/psum | solution.py:129
  100.3 3.8 %slice.20 = f32[1024,768]{1,0:T(8,128)} slice(f32[1024,1024]{1,0:T(8,128)} %all-reduce.4.cloned.1.call-done), slice={[0:1024], [0:768]} | slice | bytes 6291456 | tf_op jit(solution)/shard_map/slice | solution.py:130
  104.0 2.4 copy.9
  106.4 5.4 %gather_fusion.3 = f32[1024,1024]{1,0:T(8,128)} fusion(f32[1024,768]{0,1:T(8,128)S(1)} %copy.9, s32[1024]{0:T(1024)S(1)} %broadcast_clamp_fusion.1), kind=kCustom, calls=%fused_computation.3 | custom fusion | bytes 8392704 | tf_op jit(solution)/shard_map/jit(_take)/gather | solution.py:130
  111.8 5.4 %copy.10 = f32[1024,1024]{0,1:T(8,128)} copy(f32[1024,1024]{1,0:T(8,128)} %gather_fusion.3) | data formatting | bytes 8388608 | tf_op jit(solution)/shard_map/jit(_take)/gather | solution.py:130
  117.1 5.2 %select_bitcast_fusion.1 = f32[1024,1024]{1,0:T(8,128)} fusion(f32[1024,1024]{0,1:T(8,128)} %copy.10, pred[1024]{0:T(1024)(128)(4,1)S(1)} %get-tuple-element.11, pred[1024]{0:T(1024)(128)(4,1)S(1)} %get-tuple-element.10), kind=kLoop, calls=%fused_computation.10 | loop fusion | flops 2097152 | bytes 8390656 | tf_op jit(solution)/shard_map/jit(_where)/select_n | solution.py:130
  122.8 0.8 fusion
  123.6 158.9 %all-reduce.6.cloned.1.call-done = (f32[1536,1024]{0,1:T(8,128)}, f32[1024,1024]{1,0:T(8,128)}) async-done(((f32[1536,1024]{0,1:T(8,128)}, f32[1024,1024]{1,0:T(8,128)}), (f32[1536,1024]{0,1:T(8,128)}, f32[1024,1024]{1,0:T(8,128)})) %all-reduce.6.cloned.1.call-update) | async-done | bytes 10485776 | tf_op jit(solution)/shard_map/psum | solution.py:131
  282.5 2.2 copy-done
  284.6 62.2 %invert.1 = f32[1024,1024]{1,0:T(8,128)S(1)} custom-call(f32[1024,1024]{1,0:T(8,128)S(1)} %copy-done), custom_call_target="tpu_custom_call" | custom-call | tf_op jit(solution)/shard_map/invert/pallas_call | solution.py:102
  346.9 6.7 %fusion.5 = f32[1024,1024]{1,0:T(8,128)S(1)} fusion(f32[1024,1024]{1,0:T(8,128)S(1)} %invert.1, f32[1024,1024]{1,0:T(8,128)S(1)} %copy-done.2), kind=kOutput, calls=%fused_computation.32 | convolution fusion | flops 6442450944 | bytes 12582912 | tf_op jit(solution)/shard_map/dot_general | solution.py:113
  353.7 10.4 %fusion.6 = f32[1536,1024]{1,0:T(8,128)S(1)} fusion(f32[1536,1024]{0,1:T(8,128)S(1)} %bitcast.37, f32[1024,1024]{1,0:T(8,128)S(1)} %fusion.5), kind=kOutput, calls=%fused_computation.33 | convolution fusion | flops 9663676416 | bytes 16777216 | tf_op jit(solution)/shard_map/dot_general | solution.py:113
  364.1 1.2 fusion.4
  365.3 2.7 fusion.1
  (30 shorter events, 0.6 us)
Async XLA Ops:
  7.2 93.1 %all-reduce.4.cloned.1.call-start = ((), (), s32[]{:S(2)}) async-start(), calls=%async_computation | async-start | bytes 8388608 | tf_op jit(solution)/shard_map/psum | solution.py:129
  26.0 256.5 %all-reduce.6.cloned.1.call-start = ((), (), s32[]{:S(2)}) async-start(), calls=%async_computation.1 | async-start | bytes 20971520 | tf_op jit(solution)/shard_map/psum | solution.py:131
  282.4 2.2 copy-start
  284.6 62.2 %copy-start.2 = (f32[1024,1024]{1,0:T(8,128)S(1)}, f32[1024,1024]{1,0:T(8,128)}, u32[]{:S(2)}) copy-start(f32[1024,1024]{1,0:T(8,128)} %all-reduce.4.cloned.1.call-done) | copy-start | bytes 12582916
  284.6 69.0 %slice-start.2 = ((s8[6291456]{0:T(1024)(128)(4,1)}), s8[4194304]{0:T(1024)(128)(4,1)S(1)}, s32[]{:S(2)}) async-start(s8[6291456]{0:T(1024)(128)(4,1)} %bitcast.36), calls=%async_computation.4 | async-start | bytes 8388608
  346.9 6.8 %slice-start.3 = ((s8[6291456]{0:T(1024)(128)(4,1)}), s8[2097152]{0:T(1024)(128)(4,1)S(1)}, s32[]{:S(2)}) async-start(s8[6291456]{0:T(1024)(128)(4,1)} %bitcast.36), calls=%async_computation.5 | async-start | bytes 4194304
  346.9 18.4 %slice-start = ((s8[4718592]{0:T(1024)(128)(4,1)}), s8[4194304]{0:T(1024)(128)(4,1)S(1)}, s32[]{:S(2)}) async-start(s8[4718592]{0:T(1024)(128)(4,1)} %bitcast.26), calls=%async_computation.2 | async-start | bytes 8388608
  353.7 10.4 %copy-start.1 = (bf16[1536,256]{1,0:T(8,128)(2,1)S(1)}, bf16[1536,256]{1,0:T(8,128)(2,1)}, u32[]{:S(2)}) copy-start(bf16[1536,256]{1,0:T(8,128)(2,1)} %param.4) | copy-start | bytes 2359300
  353.7 11.6 %slice-start.1 = ((s8[4718592]{0:T(1024)(128)(4,1)}), s8[524288]{0:T(1024)(128)(4,1)S(1)}, s32[]{:S(2)}) async-start(s8[4718592]{0:T(1024)(128)(4,1)} %bitcast.26), calls=%async_computation.3 | async-start | bytes 1048576
Sparse Core Ops, SparseCore 0:
  26.1 74.1 all-reduce.3
  122.5 159.9 all-reduce.5
